TPU v7x, 256 devices: a whole 4x4x8 slice. The times are simulated.
256 devices in a mesh: space: 32 (over z, y_lo, core), tm: 4 (over x), cores: 2 (over y_hi).
Axes of the slice: x: 4, y: 4 (y_hi: 2, y_lo: 2; y = y_hi * 2 + y_lo), z: 8, core: 2. Of those that a mesh axis runs over, the one named last changes fastest.
Arguments:
- initial_state: float32 [1024, 64, 512], P('space', 'cores'), may hold values from -6 to 6
- heat_source: float32 [1024, 64, 512], P('space', 'cores'), may hold values from -3 to 3
- source_amplitude: float32 [32], P('tm'), may hold values from 0.5 to 1.5
- diffusivity: float32 [32], P('space'), may hold values from 0.5 to 2
- robin_param: float32 [32], P('space'), may hold values from 0.5 to 4
- spectrum_x: float32 [32], replicated, may hold values from 0.002 to 0.38
- spectrum_y: float32 [64], P('cores'), may hold values from 0.002 to 0.38
- spectrum_z: float32 [512], replicated, may hold values from 0.002 to 0.38
- robin_in: float32 [32, 2, 32, 64, 512], P('space', None, 'tm', 'cores'), may hold values from -8 to 8
- open_flag: int32 [32, 64], P(None, 'cores'), may hold values from 0 to 1, as said below
- owner_side: int32 [32, 64], P(None, 'cores'), may hold values from 0 to 1, as said below
Outputs:
- robin_out: float32 [32, 2, 32, 64, 512], P('space', None, 'tm', 'cores')
- window_end: float32 [4, 1024, 64, 512], P('tm', 'space', 'cores')
Inputs may be any that keep to these rules, and one draw needn't show every extreme that they name: In each aligned group of 4 modes b of an interface exactly one has open_flag 0. In each aligned pair of modes b of an interface exactly one has owner_side 1.
All inputs are finite; a program needn't handle non-finite values.
Results may differ from a plain program's by a relative error of at most 0.00015.
Values sent between devices are 32-bit elements; how exact they have to be, the bound alone decides.
A program may use at most 128 MiB of HBM per device.

v0:
```python
import jax
import jax.numpy as jnp
from jax import lax
from jax.sharding import PartitionSpec as P

HIGHEST = lax.Precision.HIGHEST


def passed_along(block, axis, distance):
    devices = range(lax.axis_size(axis))
    route = [(i - distance, i) for i in devices if i - distance in devices]
    return lax.ppermute(block, axis, route)


def passed_along_2(x, axis, by):
    devices = lax.axis_size(axis)
    return lax.ppermute(x, axis, [(i, (i + by) % devices) for i in range(devices)])


def cosine_basis(order):
    mode_rows = jnp.arange(order, dtype=jnp.float32)[:, None]
    node_cols = jnp.arange(order, dtype=jnp.float32)[None, :]
    scaling = jnp.where(mode_rows == 0, jnp.sqrt(1.0 / order), jnp.sqrt(2.0 / order))
    return scaling * jnp.cos(jnp.pi * mode_rows * (node_cols + 0.5) / order)


def local(
    initial_state,
    heat_source,
    source_amplitude,
    diffusivity,
    robin_param,
    spectrum_x,
    spectrum_y,
    spectrum_z,
    robin_in,
    open_flag,
    owner_side,
):
    nodes_x, half_y, nodes_z = initial_state.shape
    nodes_y = half_y * lax.axis_size("cores")
    core_index = lax.axis_index("cores")
    basis_x = cosine_basis(nodes_x)
    basis_y = cosine_basis(nodes_y)
    basis_z = cosine_basis(nodes_z)
    mode_block = lax.dynamic_slice_in_dim(basis_y, core_index * half_y, half_y, 0)
    node_block = lax.dynamic_slice_in_dim(basis_y, core_index * half_y, half_y, 1)

    def local_forward(values):
        values = jnp.einsum("ax,xyz->ayz", basis_x, values, precision=HIGHEST)
        return jnp.einsum("cz,ayz->ayc", basis_z, values, precision=HIGHEST)

    pieces = (
        lax.all_gather(local_forward(initial_state), "cores", axis=1, tiled=True),
        lax.all_gather(local_forward(heat_source), "cores", axis=1, tiled=True),
    )
    start_modes, source_modes = tuple(
        (
            jnp.einsum("by,ayc->abc", mode_block, piece_part, precision=HIGHEST)
            for piece_part in pieces
        )
    )
    rates = spectrum_x[:, None, None] + spectrum_y[None, :, None] + spectrum_z[None, None, :]
    factor = 1.0 / (1.0 + diffusivity[0] * rates)
    edge_rows = jnp.stack(
        [
            basis_x[:, 0],
            basis_x[:, 1] - basis_x[:, 0],
            basis_x[:, nodes_x - 1],
            basis_x[:, nodes_x - 1] - basis_x[:, nodes_x - 2],
        ]
    )
    left_col = basis_x[:, 0][:, None, None]
    right_col = basis_x[:, nodes_x - 1][:, None, None]
    robin_here = robin_in[0]
    steps_here = source_amplitude.shape[0]
    windows = lax.axis_size("tm")
    tm_index = lax.axis_index("tm")
    opening = start_modes
    for window in range(windows):
        current = opening
        collected = []
        for substep in range(steps_here):
            forcing = current
            forcing = forcing + source_amplitude[substep] * source_modes
            forcing = (
                forcing
                + left_col * robin_here[0, substep][None]
                + right_col * robin_here[1, substep][None]
            )
            current = forcing * factor
            collected.append(jnp.einsum("ka,abc->kbc", edge_rows, current, precision=HIGHEST))
        closing = current
        traces = jnp.stack(collected)
        if window + 1 < windows:
            passed = passed_along(closing, "tm", 1)
            opening = jnp.where(tm_index == 0, start_modes, passed)
    subdomains = lax.axis_size("space")
    space_index = lax.axis_index("space")
    left_index = (space_index + subdomains - 1) % subdomains
    open_right = open_flag[space_index].astype(jnp.float32)[:, None]
    open_left = open_flag[left_index].astype(jnp.float32)[:, None]
    side_right = owner_side[space_index][:, None]
    side_left = owner_side[left_index][:, None]
    owns_right = side_right == 0
    owns_left = side_left == 1
    left_face = traces[:, 0:2]
    right_face = traces[:, 2:4]
    send_left = jnp.where(side_left == 0, left_face, 0.0)
    send_right = jnp.where(side_right == 1, right_face, 0.0)
    got_right = passed_along_2(send_left, "space", -1)
    got_left = passed_along_2(send_right, "space", 1)
    own_right_data = open_right * (got_right[:, 1] + robin_param[0] * got_right[:, 0])
    own_left_data = open_left * (robin_param[0] * got_left[:, 0] - got_left[:, 1])
    back_right = jnp.where(
        owns_right, open_right * (robin_param[0] * right_face[:, 0] - right_face[:, 1]), 0.0
    )
    back_left = jnp.where(
        owns_left, open_left * (left_face[:, 1] + robin_param[0] * left_face[:, 0]), 0.0
    )
    returned_left = passed_along_2(back_right, "space", 1)
    returned_right = passed_along_2(back_left, "space", -1)
    left_data = jnp.where(owns_left, own_left_data, returned_left)
    right_data = jnp.where(owns_right, own_right_data, returned_right)
    robin_out = jnp.stack([left_data, right_data])[None]
    spectral = jnp.einsum("ax,abc->xbc", basis_x, closing, precision=HIGHEST)
    spectral = jnp.einsum("cz,xbc->xbz", basis_z, spectral, precision=HIGHEST)
    physical = jnp.einsum(
        "by,xbz->xyz",
        node_block,
        lax.all_gather(spectral, "cores", axis=1, tiled=True),
        precision=HIGHEST,
    )
    return (robin_out, physical[None])


def solution(mesh):
    placed = (
        P("space", "cores", None),
        P("space", "cores", None),
        P("tm"),
        P("space"),
        P("space"),
        P(),
        P("cores"),
        P(),
        P("space", None, "tm", "cores", None),
        P(None, "cores"),
        P(None, "cores"),
    )
    return jax.shard_map(
        local,
        mesh=mesh,
        in_specs=placed,
        out_specs=(P("space", None, "tm", "cores", None), P("tm", "space", "cores", None)),
        check_vma=False,
    )
```

profile of v0, /device:TPU:3, one launch (start us, length us, event | category | flops | bytes accessed | tf_op | source)
XLA Modules:
  0.0 476.9 jit_solution(9938863236364807262)
XLA Ops:
  7.3 1.5 copy-done
  8.8 3.1 fusion.57
  11.9 10.7 %fusion.55 = f32[32,32,512]{2,1,0:T(8,128)} fusion(f32[32,32,512]{2,0,1:T(8,128)S(1)} %fusion.57, f32[512]{0:T(512)S(1)} %get-tuple-element.57, f32[512]{0:T(512)S(1)} %get-tuple-element.58, f32[512]{0:T(512)S(1)} %fusion.181), kind=kOutput, calls=%fused_computation.133 | convolution fusion | flops 3222011904 | bytes 4200448 | tf_op jit(solution)/shard_map/cz,ayz->ayc/dot_general | solution.py:51
  23.0 4.7 fusion.61
  27.6 10.7 %fusion.59 = f32[32,32,512]{2,1,0:T(8,128)} fusion(f32[32,32,512]{2,0,1:T(8,128)S(1)} %fusion.61, f32[512]{0:T(512)S(1)} %get-tuple-element.57, f32[512]{0:T(512)S(1)} %get-tuple-element.58, f32[512]{0:T(512)S(1)} %fusion.181), kind=kOutput, calls=%fused_computation.137 | convolution fusion | flops 3222011904 | bytes 4200448 | tf_op jit(solution)/shard_map/cz,ayz->ayc/dot_general | solution.py:51
  40.9 48.2 %all-gather.6.cloned.1.call-done = f32[32,64,512]{2,1,0:T(8,128)} async-done(((f32[32,32,512]{2,1,0:T(8,128)}), f32[32,64,512]{2,1,0:T(8,128)}) %all-gather.6.cloned.1.call-update) | async-done | bytes 4194320 | tf_op jit(solution)/shard_map/all_gather | solution.py:55
  89.1 4.2 fusion.160
  93.2 60.5 %all-gather.4.cloned.1.call-done = f32[32,64,512]{2,1,0:T(8,128)} async-done(((f32[32,32,512]{2,1,0:T(8,128)}), f32[32,64,512]{2,1,0:T(8,128)}) %all-gather.4.cloned.1.call-update) | async-done | bytes 4194320 | tf_op jit(solution)/shard_map/all_gather | solution.py:54
  153.7 14.2 %fusion.49 = (f32[32,32,512]{2,1,0:T(8,128)}, f32[32,512,32]{1,2,0:T(8,128)}) fusion(f32[32,512,32]{1,2,0:T(8,128)S(1)} %fusion.160, f32[32,512]{1,0:T(8,128)S(1)} %get-tuple-element.16, f32[32,512]{1,0:T(8,128)S(1)} %get-tuple-element.17, f32[]{:T(128)} %bitcast.45, f32[32,512]{1,0:T(8,128)S(1)} %get-tuple-element.18, ...), kind=kOutput, calls=%fused_computation.113 | convolution fusion | flops 434110464 | bytes 11570216 | tf_op jit(solution)/shard_map/by,ayc->abc/dot_general | solution.py:59
  167.9 3.1 collective-permute-start
  171.0 45.6 %collective-permute-done = f32[32,32,512]{2,1,0:T(8,128)} collective-permute-done((f32[32,32,512]{2,1,0:T(8,128)}, f32[32,32,512]{2,1,0:T(8,128)}, u32[]{:S(2)}, u32[]{:S(2)}) %collective-permute-start) | collective-permute-done | bytes 2097184 | tf_op jit(solution)/shard_map/ppermute | solution.py:12
  216.6 11.1 %fusion.50 = f32[32,32,512]{2,1,0:T(8,128)S(1)} fusion(f32[32,32,512]{2,1,0:T(8,128)} %collective-permute-done, f32[32,512,32]{1,2,0:T(8,128)} %get-tuple-element.54, f32[32,512,32]{1,2,0:T(8,128)S(1)} %fusion.160, f32[32,512]{1,0:T(8,128)S(1)} %get-tuple-element.16, f32[32,512]{1,0:T(8,128)S(1)} %get-tuple-element.17, f32[]{:T(128)} %bitcast.45, ...), kind=kLoop, calls=%fused_computation.114 | loop fusion | flops 31981568 | bytes 9443621 | tf_op jit(solution)/shard_map/mul | solution.py:91
  227.7 3.1 collective-permute-start.1
  230.8 44.4 %collective-permute-done.1 = f32[32,32,512]{2,1,0:T(8,128)S(1)} collective-permute-done((f32[32,32,512]{2,1,0:T(8,128)S(1)}, f32[32,32,512]{2,1,0:T(8,128)S(1)}, u32[]{:S(2)}, u32[]{:S(2)}) %collective-permute-start.1) | collective-permute-done | bytes 2097184 | tf_op jit(solution)/shard_map/ppermute | solution.py:12
  275.2 10.5 %fusion.51 = f32[32,32,512]{2,1,0:T(8,128)} fusion(f32[32,32,512]{2,1,0:T(8,128)S(1)} %collective-permute-done.1, f32[32,512,32]{1,2,0:T(8,128)S(1)} %copy-done.4, f32[32,512,32]{1,2,0:T(8,128)S(1)} %fusion.160, f32[32,512]{1,0:T(8,128)S(1)} %get-tuple-element.16, f32[32,512]{1,0:T(8,128)S(1)} %get-tuple-element.17, f32[]{:T(128)} %bitcast.45, ...), kind=kLoop, calls=%fused_computation.115 | loop fusion | flops 31981568 | bytes 9443621 | tf_op jit(solution)/shard_map/mul | solution.py:91
  285.7 3.1 collective-permute-start.2
  291.0 41.6 %collective-permute-done.2 = f32[32,32,512]{2,1,0:T(8,128)} collective-permute-done((f32[32,32,512]{2,1,0:T(8,128)}, f32[32,32,512]{2,1,0:T(8,128)}, u32[]{:S(2)}, u32[]{:S(2)}) %collective-permute-start.2) | collective-permute-done | bytes 2097184 | tf_op jit(solution)/shard_map/ppermute | solution.py:12
  332.5 14.2 %fusion.52 = (f32[32,32,512]{2,1,0:T(8,128)S(1)}, f32[32,32,512]{2,1,0:T(8,128)}, f32[32,32,512]{2,1,0:T(8,128)}, f32[32,32,512]{2,1,0:T(8,128)}, f32[32,32,512]...) fusion(f32[32,512,32]{1,2,0:T(8,128)S(1)} %fusion.160, ...), kind=kLoop, calls=%fused_computation.116 | loop fusion | flops 31981568 | bytes 24123684 | tf_op jit(solution)/shard_map/mul | solution.py:91
  346.8 3.1 fusion.77
  349.9 9.4 %fusion.53 = f32[32,32,512]{2,1,0:T(8,128)} fusion(f32[32,32,512]{2,0,1:T(8,128)S(1)} %fusion.77, f32[512]{0:T(512)S(1)} %get-tuple-element.57, f32[512]{0:T(512)S(1)} %get-tuple-element.58, f32[512]{0:T(512)S(1)} %fusion.181), kind=kOutput, calls=%fused_computation.131 | convolution fusion | flops 3222011904 | bytes 4200448 | tf_op jit(solution)/shard_map/cz,xbc->xbz/dot_general | solution.py:127
  359.4 4.1 fusion.90
  363.5 2.3 fusion.96
  365.8 2.3 fusion.102
  368.1 2.3 fusion.108
  370.5 2.3 fusion.114
  372.8 2.7 fusion.120
  375.5 2.3 fusion.126
  377.8 2.3 fusion.84
  381.4 3.7 collective-permute-start.3
  387.5 65.4 %collective-permute-done.4 = f32[8,32,512]{2,1,0:T(8,128)S(1)} collective-permute-done((f32[8,32,512]{2,1,0:T(8,128)S(1)}, f32[8,32,512]{2,1,0:T(8,128)S(1)}, u32[]{:S(2)}, u32[]{:S(2)}) %collective-permute-start.4) | collective-permute-done | bytes 524320 | tf_op jit(solution)/shard_map/ppermute | solution.py:17
  453.6 9.3 %collective-permute-done.6 = f32[8,32,512]{2,1,0:T(8,128)S(1)} collective-permute-done((f32[8,32,512]{2,1,0:T(8,128)S(1)}, f32[8,32,512]{2,1,0:T(8,128)S(1)}, u32[]{:S(2)}, u32[]{:S(2)}) %collective-permute-start.6) | collective-permute-done | bytes 524320 | tf_op jit(solution)/shard_map/ppermute | solution.py:17
  464.2 6.0 %convolution_bitcast_fusion = f32[1,32,32,512]{3,2,1,0:T(8,128)} fusion(f32[32,64,512]{2,1,0:T(8,128)} %all-gather.8.cloned.1.call-done, f32[64,64]{1,0:T(8,128)S(1)} %cosine_multiply_fusion.4, s32[]{:T(128)S(6)} %select_n.140), kind=kOutput, calls=%fused_computation.160 | convolution fusion | flops 402653184 | bytes 6307844 | tf_op jit(solution)/shard_map/by,xbz->xyz/dot_general | solution.py:128
  (66 shorter events, 9.4 us)
Async XLA Ops:
  7.2 1.6 copy-start
  7.2 81.9 %all-gather.6.cloned.1.call-start = ((), (), s32[]{:S(2)}) async-start(), calls=%async_computation.1 | async-start | bytes 6291456 | tf_op jit(solution)/shard_map/all_gather | solution.py:55
  22.6 131.1 %all-gather.4.cloned.1.call-start = ((), (), s32[]{:S(2)}) async-start(), calls=%async_computation | async-start | bytes 6291456 | tf_op jit(solution)/shard_map/all_gather | solution.py:54
  38.3 1.3 copy-start.12
  38.3 2.1 copy-start.14
  38.3 2.1 copy-start.15
  38.3 2.4 copy-start.11
  38.4 425.8 %all-gather.8.cloned.1.call-start = ((), (), s32[]{:S(2)}) async-start(), calls=%async_computation.2 | async-start | bytes 6291456 | tf_op jit(solution)/shard_map/all_gather | solution.py:131
  40.9 112.9 %copy-start.13 = (f32[512]{0:T(512)S(1)}, f32[512]{0:T(512)}, u32[]{:S(2)}) copy-start(f32[512]{0:T(512)} %param.18) | copy-start | bytes 6148
  167.9 48.7 %collective-permute-start = (f32[32,32,512]{2,1,0:T(8,128)}, f32[32,32,512]{2,1,0:T(8,128)}, u32[]{:S(2)}, u32[]{:S(2)}) collective-permute-start(f32[32,32,512]{2,1,0:T(8,128)} %get-tuple-element.53), channel_id=1, source_target_pairs={{0,2},{2,4},{4,6},{1,3},{3,5},{5,7},{8,10},{10,12},{12,14},{9,11},... | collective-permute-start | bytes 6291464 | tf_op jit(solution)/shard_map/ppermute | solution.py:12
  216.6 58.6 %copy-start.4 = (f32[32,512,32]{1,2,0:T(8,128)S(1)}, f32[32,512,32]{1,2,0:T(8,128)}, u32[]{:S(2)}) copy-start(f32[32,512,32]{1,2,0:T(8,128)} %get-tuple-element.54) | copy-start | bytes 6291460
  227.7 47.5 %collective-permute-start.1 = (f32[32,32,512]{2,1,0:T(8,128)S(1)}, f32[32,32,512]{2,1,0:T(8,128)S(1)}, u32[]{:S(2)}, u32[]{:S(2)}) collective-permute-start(f32[32,32,512]{2,1,0:T(8,128)S(1)} %fusion.50), channel_id=1, source_target_pairs={{0,2},{2,4},{4,6},{1,3},{3,5},{5,7},{8,10},{10,12},{12,14},{9,11},... | collective-permute-start | bytes 6291464 | tf_op jit(solution)/shard_map/ppermute | solution.py:12
  285.7 46.9 %collective-permute-start.2 = (f32[32,32,512]{2,1,0:T(8,128)}, f32[32,32,512]{2,1,0:T(8,128)}, u32[]{:S(2)}, u32[]{:S(2)}) collective-permute-start(f32[32,32,512]{2,1,0:T(8,128)} %fusion.51), channel_id=1, source_target_pairs={{0,2},{2,4},{4,6},{1,3},{3,5},{5,7},{8,10},{10,12},{12,14},{9,11},... | collective-permute-start | bytes 6291464 | tf_op jit(solution)/shard_map/ppermute | solution.py:12
  346.7 3.1 copy-start.2
  359.3 4.2 copy-start.10
  359.3 6.5 %copy-start.9 = (f32[32,32,512]{2,1,0:T(8,128)S(1)}, f32[32,32,512]{2,1,0:T(8,128)}, u32[]{:S(2)}) copy-start(f32[32,32,512]{2,1,0:T(8,128)} %get-tuple-element.7) | copy-start | bytes 6291460
  363.5 4.6 copy-start.8
  365.8 4.6 copy-start.7
  368.1 4.6 copy-start.6
  370.5 5.0 %copy-start.5 = (f32[32,32,512]{2,1,0:T(8,128)S(1)}, f32[32,32,512]{2,1,0:T(8,128)}, u32[]{:S(2)}) copy-start(f32[32,32,512]{2,1,0:T(8,128)} %get-tuple-element.3) | copy-start | bytes 6291460
  372.8 5.0 %copy-start.3 = (f32[32,32,512]{2,1,0:T(8,128)S(1)}, f32[32,32,512]{2,1,0:T(8,128)}, u32[]{:S(2)}) copy-start(f32[32,32,512]{2,1,0:T(8,128)} %copy-done.2) | copy-start | bytes 6291460
  381.4 71.5 %collective-permute-start.3 = (f32[8,2,32,512]{3,2,0,1:T(8,128)S(1)}, f32[8,2,32,512]{3,2,0,1:T(8,128)S(1)}, u32[]{:S(2)}, u32[]{:S(2)}) collective-permute-start(f32[8,2,32,512]{3,2,0,1:T(8,128)S(1)} %copy_select_fusion.1), channel_id=1, source_target_pairs={{0,8},{8,16},{16,24},{24,32},{32,40},{40,48},{48,56},{56,64},{64,7... | collective-permute-start | bytes 3145736 | tf_op jit(solution)/shard_map/ppermute | solution.py:17
  386.6 66.4 %collective-permute-start.4 = (f32[8,32,512]{2,1,0:T(8,128)S(1)}, f32[8,32,512]{2,1,0:T(8,128)S(1)}, u32[]{:S(2)}, u32[]{:S(2)}) collective-permute-start(f32[8,32,512]{2,1,0:T(8,128)S(1)} %fusion.144), channel_id=1, source_target_pairs={{0,8},{8,16},{16,24},{24,32},{32,40},{40,48},{48,56},{56,64},{64,7... | collective-permute-start | bytes 1572872 | tf_op jit(solution)/shard_map/ppermute | solution.py:17
  387.0 66.6 %collective-permute-start.5 = (f32[8,2,32,512]{3,2,0,1:T(8,128)S(1)}, f32[8,2,32,512]{3,2,0,1:T(8,128)S(1)}, u32[]{:S(2)}, u32[]{:S(2)}) collective-permute-start(f32[8,2,32,512]{3,2,0,1:T(8,128)S(1)} %copy_select_fusion), channel_id=1, source_target_pairs={{0,248},{8,0},{16,8},{24,16},{32,24},{40,32},{48,40},{56,48},{64,5... | collective-permute-start | bytes 3145736 | tf_op jit(solution)/shard_map/ppermute | solution.py:17
  453.3 9.6 %collective-permute-start.6 = (f32[8,32,512]{2,1,0:T(8,128)S(1)}, f32[8,32,512]{2,1,0:T(8,128)S(1)}, u32[]{:S(2)}, u32[]{:S(2)}) collective-permute-start(f32[8,32,512]{2,1,0:T(8,128)S(1)} %get-tuple-element.44), channel_id=1, source_target_pairs={{0,248},{8,0},{16,8},{24,16},{32,24},{40,32},{48,40},{56,48},{64,5... | collective-permute-start | bytes 1572872 | tf_op jit(solution)/shard_map/ppermute | solution.py:17
  463.1 7.1 %copy-start.1 = (f32[32,32,512]{2,1,0:T(8,128)S(1)}, f32[32,32,512]{2,1,0:T(8,128)}, u32[]{:S(2)}) copy-start(f32[32,32,512]{2,1,0:T(8,128)} %param.12) | copy-start | bytes 6291460
Sparse Core Ops, SparseCore 0:
  22.8 66.2 all-gather.5
  90.8 62.8 all-gather.3
  359.5 99.1 all-gather.7
where the time goes:
time: 484 us; the launch traced here: 477 us
  waiting for transfers between devices  315 us (65%)
  matrix products  86.7 us (18%)
  other arithmetic  41.4 us (9%)
  between operations  15.7 us (3%)
  starting transfers between devices  14.7 us (3%)
    ppermute x3, waiting for transfers between devices, passed_along(): return lax.ppermute(block, axis, route)  132 us
    ppermute x4, waiting for transfers between devices, passed_along_2(): lax.ppermute(x, axis, [(i, (i + by) % devices) for i in range(devices)])  74.8 us
    all_gather x1, waiting for transfers between devices, local(): lax.all_gather(local_forward(initial_state), 'cores', axis=1, tiled=True)  60.5 us
    all_gather x1, waiting for transfers between devices, local(): lax.all_gather(local_forward(heat_source), 'cores', axis=1, tiled=True)  48.2 us
    mul x3, other arithmetic, local(): current = forcing * factor  35.8 us
    dot_general x2, matrix products, local_forward(): return jnp.einsum('cz,ayz->ayc', basis_z, values, precision=HIGHEST)  21.4 us
    dot_general x8, matrix products, local(): jnp.einsum('ka,abc->kbc', edge_rows, current, precision=HIGHEST)  20.6 us
    dot_general x2, matrix products, local(): jnp.einsum('by,ayc->abc', mode_block, piece_part, precision=HIGHEST)  18.3 us
  transfers between devices with their start and end apart: 10, of which 7 were waited for; matrix products, arithmetic and copies ran while one was open for 10% of the time, Pallas kernels for 0%

commit v1 on v0

--- a/solution.py
+++ b/solution.py
@@ -51,7 +51,12 @@
         return jnp.einsum("cz,ayz->ayc", basis_z, values, precision=HIGHEST)
 
     pieces = (
-        lax.all_gather(local_forward(initial_state), "cores", axis=1, tiled=True),
+        jnp.concatenate(
+            lax.all_to_all(
+                jnp.stack([local_forward(initial_state)] * lax.axis_size("cores")), "cores", 0, 0
+            ),
+            axis=1,
+        ),
         lax.all_gather(local_forward(heat_source), "cores", axis=1, tiled=True),
     )
     start_modes, source_modes = tuple(

time: 484 us -> 473 us (0.977)
  waiting for transfers between devices: 315 us -> 293 us
  local copies, waits for them, and re-layouts: 3.34 us -> 9.94 us
  starting transfers between devices: 14.7 us -> 20.6 us
  matrix products: 86.7 us -> 81.5 us
    all_to_all x0 -> x1, waiting for transfers between devices: none -> 87.1 us  [local(): lax.all_to_all(jnp.stack([local_forward(initial_state)] * lax.axis_size('...]
    all_gather x1 -> x0, waiting for transfers between devices: 60.5 us -> none  [local(): lax.all_gather(local_forward(initial_state), 'cores', axis=1, tiled=True)]
    all_gather x1, waiting for transfers between devices: 48.2 us -> 0.01 us  [local(): lax.all_gather(local_forward(heat_source), 'cores', axis=1, tiled=True)]
    all_to_all x0 -> x1, starting transfers between devices: none -> 5.99 us  [local(): lax.all_to_all(jnp.stack([local_forward(initial_state)] * lax.axis_size('...]
    reshape x0 -> x1, local copies, waits for them, and re-layouts: none -> 5.04 us  [local(): jnp.concatenate(lax.all_to_all(jnp.stack([local_forward(initial_state)] *...]
  transfers between devices with their start and end apart: 10 -> 10, of which waited for: 7 -> 6; matrix products, arithmetic and copies ran while one was open for 10% -> 10% of each run, Pallas kernels for 0% -> 0%
where the time goes in v1:
time: 473 us; the launch traced here: 466 us
  waiting for transfers between devices  293 us (62%)
  matrix products  81.5 us (17%)
  other arithmetic  44.7 us (9%)
  starting transfers between devices  20.6 us (4%)
  between operations  16 us (3%)
  local copies, waits for them, and re-layouts  9.94 us (2%)
    ppermute x3, waiting for transfers between devices, passed_along(): return lax.ppermute(block, axis, route)  131 us
    all_to_all x1, waiting for transfers between devices, local(): lax.all_to_all(jnp.stack([local_forward(initial_state)] * lax.axis_size('...  87.1 us
    ppermute x4, waiting for transfers between devices, passed_along_2(): lax.ppermute(x, axis, [(i, (i + by) % devices) for i in range(devices)])  74.8 us
    mul x3, other arithmetic, local(): current = forcing * factor  36.3 us
    dot_general x8, matrix products, local(): jnp.einsum('ka,abc->kbc', edge_rows, current, precision=HIGHEST)  20.6 us
    dot_general x2, matrix products, local_forward(): return jnp.einsum('cz,ayz->ayc', basis_z, values, precision=HIGHEST)  19.2 us
    dot_general x2, matrix products, local(): jnp.einsum('by,ayc->abc', mode_block, piece_part, precision=HIGHEST)  17 us
  transfers between devices with their start and end apart: 10, of which 6 were waited for; matrix products, arithmetic and copies ran while one was open for 10% of the time, Pallas kernels for 0%

profile of v1, /device:TPU:3, one launch (start us, length us, event | category | flops | bytes accessed | tf_op | source)
XLA Modules:
  0.0 465.8 jit_solution(14394723024580338765)
XLA Ops:
  8.8 3.1 fusion.57
  11.9 11.0 %fusion.55 = f32[32,32,512]{2,1,0:T(8,128)} fusion(f32[32,32,512]{2,0,1:T(8,128)S(1)} %fusion.57, f32[512]{0:T(512)S(1)} %get-tuple-element.57, f32[512]{0:T(512)S(1)} %get-tuple-element.58, f32[512]{0:T(512)S(1)} %fusion.184), kind=kOutput, calls=%fused_computation.134 | convolution fusion | flops 3222011904 | bytes 4200448 | tf_op jit(solution)/shard_map/cz,ayz->ayc/dot_general | solution.py:51
  24.5 3.1 fusion.61
  27.6 8.2 %fusion.81 = f32[1,32,32,512]{3,2,1,0:T(8,128)S(1)} fusion(f32[32,32,512]{2,0,1:T(8,128)S(1)} %fusion.61, f32[512]{0:T(512)S(1)} %get-tuple-element.57, f32[512]{0:T(512)S(1)} %get-tuple-element.58, f32[512]{0:T(512)S(1)} %fusion.184), kind=kOutput, calls=%fused_computation.161 | convolution fusion | flops 3222011904 | bytes 4200448 | tf_op jit(solution)/shard_map/cz,ayz->ayc/dot_general | solution.py:51
  35.8 2.7 pad_maximum_fusion
  38.5 6.0 %all-to-all-start = ((f32[2,32,32,512]{3,2,1,0:T(8,128)}), f32[2,32,32,512]{3,2,1,0:T(8,128)}, u32[]{:S(2)}, u32[]{:S(2)}) async-start(f32[2,32,32,512]{3,2,1,0:T(8,128)} %pad_maximum_fusion), calls=%async_computation | async-start | bytes 8388608 | tf_op jit(solution)/shard_map/all_to_all | solution.py:55
  47.0 87.1 %all-to-all-done = f32[2,32,32,512]{3,2,1,0:T(8,128)} async-done(((f32[2,32,32,512]{3,2,1,0:T(8,128)}), f32[2,32,32,512]{3,2,1,0:T(8,128)}, u32[]{:S(2)}, u32[]{:S(2)}) %all-to-all-start) | async-done | bytes 4194336 | tf_op jit(solution)/shard_map/all_to_all | solution.py:55
  134.1 5.0 %copy.27 = f32[32,2,32,512]{3,2,1,0:T(8,128)} copy(f32[32,2,32,512]{3,2,0,1:T(8,128)} %bitcast.12) | data formatting | bytes 8388608 | tf_op jit(solution)/shard_map/reshape | solution.py:54
  139.2 4.3 fusion.163
  143.5 12.7 %fusion.49 = (f32[32,32,512]{2,1,0:T(8,128)}, f32[32,512,32]{1,2,0:T(8,128)}) fusion(f32[32,512,32]{1,2,0:T(8,128)S(1)} %fusion.163, f32[32,512]{1,0:T(8,128)S(1)} %get-tuple-element.16, f32[32,512]{1,0:T(8,128)S(1)} %get-tuple-element.17, f32[]{:T(128)} %bitcast.48, f32[32,512]{1,0:T(8,128)S(1)} %get-tuple-element.18, ...), kind=kOutput, calls=%fused_computation.114 | convolution fusion | flops 434110464 | bytes 11570216 | tf_op jit(solution)/shard_map/by,ayc->abc/dot_general | solution.py:64
  156.2 3.1 collective-permute-start
  159.3 45.5 %collective-permute-done = f32[32,32,512]{2,1,0:T(8,128)} collective-permute-done((f32[32,32,512]{2,1,0:T(8,128)}, f32[32,32,512]{2,1,0:T(8,128)}, u32[]{:S(2)}, u32[]{:S(2)}) %collective-permute-start) | collective-permute-done | bytes 2097184 | tf_op jit(solution)/shard_map/ppermute | solution.py:12
  204.8 11.3 %fusion.50 = f32[32,32,512]{2,1,0:T(8,128)S(1)} fusion(f32[32,32,512]{2,1,0:T(8,128)} %collective-permute-done, f32[32,512,32]{1,2,0:T(8,128)} %get-tuple-element.54, f32[32,512,32]{1,2,0:T(8,128)S(1)} %fusion.163, f32[32,512]{1,0:T(8,128)S(1)} %get-tuple-element.16, f32[32,512]{1,0:T(8,128)S(1)} %get-tuple-element.17, f32[]{:T(128)} %bitcast.48, ...), kind=kLoop, calls=%fused_computation.115 | loop fusion | flops 31981568 | bytes 9443621 | tf_op jit(solution)/shard_map/mul | solution.py:96
  216.1 3.1 collective-permute-start.1
  219.2 44.3 %collective-permute-done.1 = f32[32,32,512]{2,1,0:T(8,128)S(1)} collective-permute-done((f32[32,32,512]{2,1,0:T(8,128)S(1)}, f32[32,32,512]{2,1,0:T(8,128)S(1)}, u32[]{:S(2)}, u32[]{:S(2)}) %collective-permute-start.1) | collective-permute-done | bytes 2097184 | tf_op jit(solution)/shard_map/ppermute | solution.py:12
  263.5 10.7 %fusion.51 = f32[32,32,512]{2,1,0:T(8,128)} fusion(f32[32,32,512]{2,1,0:T(8,128)S(1)} %collective-permute-done.1, f32[32,512,32]{1,2,0:T(8,128)S(1)} %copy-done.4, f32[32,512,32]{1,2,0:T(8,128)S(1)} %fusion.163, f32[32,512]{1,0:T(8,128)S(1)} %get-tuple-element.16, f32[32,512]{1,0:T(8,128)S(1)} %get-tuple-element.17, f32[]{:T(128)} %bitcast.48, ...), kind=kLoop, calls=%fused_computation.116 | loop fusion | flops 31981568 | bytes 9443621 | tf_op jit(solution)/shard_map/mul | solution.py:96
  274.1 3.1 collective-permute-start.2
  279.4 41.4 %collective-permute-done.2 = f32[32,32,512]{2,1,0:T(8,128)} collective-permute-done((f32[32,32,512]{2,1,0:T(8,128)}, f32[32,32,512]{2,1,0:T(8,128)}, u32[]{:S(2)}, u32[]{:S(2)}) %collective-permute-start.2) | collective-permute-done | bytes 2097184 | tf_op jit(solution)/shard_map/ppermute | solution.py:12
  320.9 14.4 %fusion.52 = (f32[32,32,512]{2,1,0:T(8,128)S(1)}, f32[32,32,512]{2,1,0:T(8,128)}, f32[32,32,512]{2,1,0:T(8,128)}, f32[32,32,512]{2,1,0:T(8,128)}, f32[32,32,512]...) fusion(f32[32,512,32]{1,2,0:T(8,128)S(1)} %fusion.163, ...), kind=kLoop, calls=%fused_computation.117 | loop fusion | flops 31981568 | bytes 24123684 | tf_op jit(solution)/shard_map/mul | solution.py:96
  335.3 3.1 fusion.77
  338.4 9.4 %fusion.53 = f32[32,32,512]{2,1,0:T(8,128)} fusion(f32[32,32,512]{2,0,1:T(8,128)S(1)} %fusion.77, f32[512]{0:T(512)S(1)} %get-tuple-element.57, f32[512]{0:T(512)S(1)} %get-tuple-element.58, f32[512]{0:T(512)S(1)} %fusion.184), kind=kOutput, calls=%fused_computation.132 | convolution fusion | flops 3222011904 | bytes 4200448 | tf_op jit(solution)/shard_map/cz,xbc->xbz/dot_general | solution.py:132
  347.8 4.1 fusion.93
  352.0 2.3 fusion.99
  354.3 2.3 fusion.105
  356.6 2.3 fusion.111
  358.9 2.3 fusion.117
  361.3 2.7 fusion.123
  364.0 2.3 fusion.129
  369.9 3.8 collective-permute-start.3
  376.2 65.4 %collective-permute-done.4 = f32[8,32,512]{2,1,0:T(8,128)S(1)} collective-permute-done((f32[8,32,512]{2,1,0:T(8,128)S(1)}, f32[8,32,512]{2,1,0:T(8,128)S(1)}, u32[]{:S(2)}, u32[]{:S(2)}) %collective-permute-start.4) | collective-permute-done | bytes 524320 | tf_op jit(solution)/shard_map/ppermute | solution.py:17
  442.2 9.3 %collective-permute-done.6 = f32[8,32,512]{2,1,0:T(8,128)S(1)} collective-permute-done((f32[8,32,512]{2,1,0:T(8,128)S(1)}, f32[8,32,512]{2,1,0:T(8,128)S(1)}, u32[]{:S(2)}, u32[]{:S(2)}) %collective-permute-start.6) | collective-permute-done | bytes 524320 | tf_op jit(solution)/shard_map/ppermute | solution.py:17
  452.8 6.0 %convolution_bitcast_fusion = f32[1,32,32,512]{3,2,1,0:T(8,128)} fusion(f32[32,64,512]{2,1,0:T(8,128)} %all-gather.5.cloned.1.call-done, f32[64,64]{1,0:T(8,128)S(1)} %cosine_multiply_fusion.4, s32[]{:T(128)S(6)} %select_n.140), kind=kOutput, calls=%fused_computation.162 | convolution fusion | flops 402653184 | bytes 6307844 | tf_op jit(solution)/shard_map/by,xbz->xyz/dot_general | solution.py:133
  (71 shorter events, 14.4 us)
Async XLA Ops:
  7.2 1.6 copy-start
  7.2 132.0 %all-gather.3.cloned.1.call-start = ((), (), s32[]{:S(2)}) async-start(), calls=%async_computation.1 | async-start | bytes 6291456 | tf_op jit(solution)/shard_map/all_gather | solution.py:60
  22.9 1.6 copy-start.12
  38.5 7.3 %copy-start.14 = (f32[8]{0:T(128)S(1)}, f32[8]{0:T(128)}, u32[]{:S(2)}) copy-start(f32[8]{0:T(128)} %param.13) | copy-start | bytes 100
  38.5 8.1 %copy-start.16 = (f32[32]{0:T(128)S(1)}, f32[32]{0:T(128)}, u32[]{:S(2)}) copy-start(f32[32]{0:T(128)} %param.17) | copy-start | bytes 388
  38.5 8.1 %copy-start.17 = (f32[32]{0:T(128)S(1)}, f32[32]{0:T(128)}, u32[]{:S(2)}) copy-start(f32[32]{0:T(128)} %param.16) | copy-start | bytes 388
  38.5 8.4 %copy-start.13 = (f32[1,2,8,32,512]{4,3,2,1,0:T(8,128)S(1)}, f32[1,2,8,32,512]{4,3,2,1,0:T(8,128)}, u32[]{:S(2)}) copy-start(f32[1,2,8,32,512]{4,3,2,1,0:T(8,128)} %param.19) | copy-start | bytes 3145732
  38.5 95.6 %all-to-all-start = ((f32[2,32,32,512]{3,2,1,0:T(8,128)}), f32[2,32,32,512]{3,2,1,0:T(8,128)}, u32[]{:S(2)}, u32[]{:S(2)}) async-start(f32[2,32,32,512]{3,2,1,0:T(8,128)} %pad_maximum_fusion), calls=%async_computation | async-start | bytes 8388608 | tf_op jit(solution)/shard_map/all_to_all | solution.py:55
  44.5 408.3 %all-gather.5.cloned.1.call-start = ((), (), s32[]{:S(2)}) async-start(), calls=%async_computation.2 | async-start | bytes 6291456 | tf_op jit(solution)/shard_map/all_gather | solution.py:136
  139.2 4.3 copy-start.15
  139.2 4.3 copy-start.11
  156.2 48.6 %collective-permute-start = (f32[32,32,512]{2,1,0:T(8,128)}, f32[32,32,512]{2,1,0:T(8,128)}, u32[]{:S(2)}, u32[]{:S(2)}) collective-permute-start(f32[32,32,512]{2,1,0:T(8,128)} %get-tuple-element.53), channel_id=1, source_target_pairs={{0,2},{2,4},{4,6},{1,3},{3,5},{5,7},{8,10},{10,12},{12,14},{9,11},... | collective-permute-start | bytes 6291464 | tf_op jit(solution)/shard_map/ppermute | solution.py:12
  204.8 58.7 %copy-start.4 = (f32[32,512,32]{1,2,0:T(8,128)S(1)}, f32[32,512,32]{1,2,0:T(8,128)}, u32[]{:S(2)}) copy-start(f32[32,512,32]{1,2,0:T(8,128)} %get-tuple-element.54) | copy-start | bytes 6291460
  216.1 47.4 %collective-permute-start.1 = (f32[32,32,512]{2,1,0:T(8,128)S(1)}, f32[32,32,512]{2,1,0:T(8,128)S(1)}, u32[]{:S(2)}, u32[]{:S(2)}) collective-permute-start(f32[32,32,512]{2,1,0:T(8,128)S(1)} %fusion.50), channel_id=1, source_target_pairs={{0,2},{2,4},{4,6},{1,3},{3,5},{5,7},{8,10},{10,12},{12,14},{9,11},... | collective-permute-start | bytes 6291464 | tf_op jit(solution)/shard_map/ppermute | solution.py:12
  274.1 46.8 %collective-permute-start.2 = (f32[32,32,512]{2,1,0:T(8,128)}, f32[32,32,512]{2,1,0:T(8,128)}, u32[]{:S(2)}, u32[]{:S(2)}) collective-permute-start(f32[32,32,512]{2,1,0:T(8,128)} %fusion.51), channel_id=1, source_target_pairs={{0,2},{2,4},{4,6},{1,3},{3,5},{5,7},{8,10},{10,12},{12,14},{9,11},... | collective-permute-start | bytes 6291464 | tf_op jit(solution)/shard_map/ppermute | solution.py:12
  335.3 3.1 copy-start.2
  347.8 4.2 copy-start.10
  347.8 6.5 %copy-start.9 = (f32[32,32,512]{2,1,0:T(8,128)S(1)}, f32[32,32,512]{2,1,0:T(8,128)}, u32[]{:S(2)}) copy-start(f32[32,32,512]{2,1,0:T(8,128)} %get-tuple-element.7) | copy-start | bytes 6291460
  352.0 4.6 copy-start.8
  354.3 4.6 copy-start.7
  356.6 4.6 copy-start.6
  358.9 5.0 %copy-start.5 = (f32[32,32,512]{2,1,0:T(8,128)S(1)}, f32[32,32,512]{2,1,0:T(8,128)}, u32[]{:S(2)}) copy-start(f32[32,32,512]{2,1,0:T(8,128)} %get-tuple-element.3) | copy-start | bytes 6291460
  361.3 5.0 %copy-start.3 = (f32[32,32,512]{2,1,0:T(8,128)S(1)}, f32[32,32,512]{2,1,0:T(8,128)}, u32[]{:S(2)}) copy-start(f32[32,32,512]{2,1,0:T(8,128)} %copy-done.2) | copy-start | bytes 6291460
  369.9 71.7 %collective-permute-start.3 = (f32[8,2,32,512]{3,2,0,1:T(8,128)S(1)}, f32[8,2,32,512]{3,2,0,1:T(8,128)S(1)}, u32[]{:S(2)}, u32[]{:S(2)}) collective-permute-start(f32[8,2,32,512]{3,2,0,1:T(8,128)S(1)} %copy_select_fusion.1), channel_id=1, source_target_pairs={{0,8},{8,16},{16,24},{24,32},{32,40},{40,48},{48,56},{56,64},{64,7... | collective-permute-start | bytes 3145736 | tf_op jit(solution)/shard_map/ppermute | solution.py:17
  375.2 66.4 %collective-permute-start.4 = (f32[8,32,512]{2,1,0:T(8,128)S(1)}, f32[8,32,512]{2,1,0:T(8,128)S(1)}, u32[]{:S(2)}, u32[]{:S(2)}) collective-permute-start(f32[8,32,512]{2,1,0:T(8,128)S(1)} %fusion.147), channel_id=1, source_target_pairs={{0,8},{8,16},{16,24},{24,32},{32,40},{40,48},{48,56},{56,64},{64,7... | collective-permute-start | bytes 1572872 | tf_op jit(solution)/shard_map/ppermute | solution.py:17
  375.6 66.6 %collective-permute-start.5 = (f32[8,2,32,512]{3,2,0,1:T(8,128)S(1)}, f32[8,2,32,512]{3,2,0,1:T(8,128)S(1)}, u32[]{:S(2)}, u32[]{:S(2)}) collective-permute-start(f32[8,2,32,512]{3,2,0,1:T(8,128)S(1)} %copy_select_fusion), channel_id=1, source_target_pairs={{0,248},{8,0},{16,8},{24,16},{32,24},{40,32},{48,40},{56,48},{64,5... | collective-permute-start | bytes 3145736 | tf_op jit(solution)/shard_map/ppermute | solution.py:17
  441.9 9.6 %collective-permute-start.6 = (f32[8,32,512]{2,1,0:T(8,128)S(1)}, f32[8,32,512]{2,1,0:T(8,128)S(1)}, u32[]{:S(2)}, u32[]{:S(2)}) collective-permute-start(f32[8,32,512]{2,1,0:T(8,128)S(1)} %get-tuple-element.44), channel_id=1, source_target_pairs={{0,248},{8,0},{16,8},{24,16},{32,24},{40,32},{48,40},{56,48},{64,5... | collective-permute-start | bytes 1572872 | tf_op jit(solution)/shard_map/ppermute | solution.py:17
  451.7 7.1 %copy-start.1 = (f32[32,32,512]{2,1,0:T(8,128)S(1)}, f32[32,32,512]{2,1,0:T(8,128)}, u32[]{:S(2)}) copy-start(f32[32,32,512]{2,1,0:T(8,128)} %param.12) | copy-start | bytes 6291460
Sparse Core Ops, SparseCore 0:
  23.0 106.2 all-gather.2
  347.9 99.5 all-gather.4
